TPU v7x, 256 devices: a whole 4x4x8 slice. The times are simulated.
256 devices in a mesh: dp: 2 (over core), row: 16 (over x, y), col: 8 (over z).
Axes of the slice: x: 4, y: 4, z: 8, core: 2. Of those that a mesh axis runs over, the one named last changes fastest.
Arguments:
- tokens: bfloat16 [768, 8192], P(('dp', 'col'), 'row'), may hold values from -160 to 160
- norm_gain: float32 [8192], P('row'), may hold values from 0.3 to 3
- gate_weight: bfloat16 [8192, 14336], P('row', ('dp', 'col')), may hold values from -0.0625 to 0.0625
- up_weight: bfloat16 [8192, 14336], P('row', ('dp', 'col')), may hold values from -0.0625 to 0.0625
- down_weight: bfloat16 [14336, 8192], P(('dp', 'col'), 'row'), may hold values from -0.046875 to 0.046875
- gate_keep: int32 [64, 112], P('row', ('dp', 'col')), may hold values from 0 to 1, as said below
- up_keep: int32 [64, 112], P('row', ('dp', 'col')), may hold values from 0 to 1, as said below
- down_keep: int32 [112, 64], P(('dp', 'col'), 'row'), may hold values from 0 to 1, as said below
- cotangent: bfloat16 [768, 8192], P(('dp', 'col'), 'row'), may hold values from -80 to 80
Outputs:
- branch: bfloat16 [768, 8192], P(('dp', 'col'), 'row')
- grad_tokens: float32 [768, 8192], P(('dp', 'col'), 'row')
- grad_gain: float32 [8192], P('row')
- grad_gate: float32 [8192, 14336], P('row', ('dp', 'col'))
- grad_up: float32 [8192, 14336], P('row', ('dp', 'col'))
- grad_down: float32 [14336, 8192], P(('dp', 'col'), 'row')
Inputs may be any that keep to these rules, and one draw needn't show every extreme that they name: `gate_keep`: 1 keeps a 128 x 128 block of the gate projection, 0 prunes it. `up_keep`: 1 keeps a 128 x 128 block of the up projection, 0 prunes it. `down_keep`: 1 keeps a 128 x 128 block of the down projection, 0 prunes it.
All inputs are finite; a program needn't handle non-finite values.
Results may differ from a plain program's by a relative error of at most 0.0065.
Values may be sent and summed in bfloat16 or wider, within the bound.
A program may use at most 128 MiB of HBM per device.

v0:
```python
import jax
import jax.numpy as jnp
from jax import lax
from jax.sharding import PartitionSpec as P

D = 8192
BLOCK = 128


def expand_keep(keep, target_type):
    return jnp.repeat(jnp.repeat(keep, BLOCK, axis=0), BLOCK, axis=1).astype(target_type)


def activate(gate, up_value):
    return (gate * jax.nn.sigmoid(gate) * up_value).astype(jnp.bfloat16)


def on_device(
    tokens, norm_gain, gate_weight, up_weight, down_weight, gate_keep, up_keep, down_keep, cotangent
):
    token_f = tokens.astype(jnp.float32)
    square = lax.psum(jnp.sum(token_f * token_f, axis=1), "row")
    inv_rms = lax.rsqrt(square[:, None] / D + 1e-05)
    normed = (token_f * inv_rms * norm_gain).astype(jnp.bfloat16)
    gate_masked = gate_weight * expand_keep(gate_keep, jnp.bfloat16)
    up_masked = up_weight * expand_keep(up_keep, jnp.bfloat16)
    down_masked = down_weight * expand_keep(down_keep, jnp.bfloat16)
    gate_full, up_full = (
        lax.all_gather(gate_masked, "dp", axis=1, tiled=True),
        lax.all_gather(up_masked, "dp", axis=1, tiled=True),
    )
    down_full = lax.all_gather(down_masked, "dp", axis=0, tiled=True)
    seen_rows = lax.all_gather(normed, "col", axis=0, tiled=True)
    seen_cot = lax.all_gather(cotangent, "col", axis=0, tiled=True)
    width_f = gate_full.shape[1]
    contract_last = (((1,), (1,)), ((), ()))
    contract_first = (((0,), (0,)), ((), ()))
    row_block = seen_rows
    summed = lax.psum_scatter(
        jnp.concatenate(
            [
                jnp.dot(row_block, gate_full, preferred_element_type=jnp.float32),
                jnp.dot(row_block, up_full, preferred_element_type=jnp.float32),
            ],
            axis=1,
        ),
        "row",
        scatter_dimension=0,
        tiled=True,
    )
    gate_part = summed[:, :width_f]
    up_part = summed[:, width_f:]
    hidden = lax.all_gather(activate(gate_part, up_part), "row", axis=0, tiled=True)
    row_block = hidden
    branch_sum = lax.psum_scatter(
        jnp.dot(row_block, down_full, preferred_element_type=jnp.float32),
        "col",
        scatter_dimension=0,
        tiled=True,
    )
    branch = branch_sum.astype(jnp.bfloat16)
    row_block = seen_cot
    hidden_grad = lax.psum_scatter(
        lax.dot_general(row_block, down_full, contract_last, preferred_element_type=jnp.float32),
        "row",
        scatter_dimension=0,
        tiled=True,
    )
    sigmoid_gate = jax.nn.sigmoid(gate_part)
    gate_grad = (
        hidden_grad * up_part * sigmoid_gate * (1.0 + gate_part * (1.0 - sigmoid_gate))
    ).astype(jnp.bfloat16)
    up_grad = (hidden_grad * gate_part * sigmoid_gate).astype(jnp.bfloat16)
    gate_grads, up_grads = (
        lax.all_gather(gate_grad, "row", axis=0, tiled=True),
        lax.all_gather(up_grad, "row", axis=0, tiled=True),
    )
    normed_grad = lax.psum_scatter(
        lax.dot_general(gate_grads, gate_full, contract_last, preferred_element_type=jnp.float32)
        + lax.dot_general(up_grads, up_full, contract_last, preferred_element_type=jnp.float32),
        "col",
        scatter_dimension=0,
        tiled=True,
    )
    down_local = lax.dot_general(
        hidden, seen_cot, contract_first, preferred_element_type=jnp.float32
    )
    gate_local = lax.dot_general(
        seen_rows, gate_grads, contract_first, preferred_element_type=jnp.float32
    )
    up_local = lax.dot_general(
        seen_rows, up_grads, contract_first, preferred_element_type=jnp.float32
    )
    gate_total, up_total = (
        lax.psum_scatter(gate_local, "dp", scatter_dimension=1, tiled=True),
        lax.psum_scatter(up_local, "dp", scatter_dimension=1, tiled=True),
    )
    down_total = lax.psum_scatter(down_local, "dp", scatter_dimension=0, tiled=True)
    grad_gate = gate_total * expand_keep(gate_keep, jnp.float32)
    grad_up = up_total * expand_keep(up_keep, jnp.float32)
    grad_down = down_total * expand_keep(down_keep, jnp.float32)
    grad_gain = lax.psum(jnp.sum(normed_grad * token_f * inv_rms, axis=0), ("dp", "col"))
    inner_dot = lax.psum(jnp.sum(norm_gain * normed_grad * token_f, axis=1), "row")
    grad_tokens = (
        inv_rms * norm_gain * normed_grad
        - token_f * inv_rms * inv_rms * inv_rms * inner_dot[:, None] / D
    )
    return (branch, grad_tokens, grad_gain, grad_gate, grad_up, grad_down)


def solution(mesh):
    in_specs = (
        P(("dp", "col"), "row"),
        P("row"),
        P("row", ("dp", "col")),
        P("row", ("dp", "col")),
        P(("dp", "col"), "row"),
        P("row", ("dp", "col")),
        P("row", ("dp", "col")),
        P(("dp", "col"), "row"),
        P(("dp", "col"), "row"),
    )
    out_specs = (
        P(("dp", "col"), "row"),
        P(("dp", "col"), "row"),
        P("row"),
        P("row", ("dp", "col")),
        P("row", ("dp", "col")),
        P(("dp", "col"), "row"),
    )
    return jax.shard_map(
        on_device, mesh=mesh, in_specs=in_specs, out_specs=out_specs, check_vma=False
    )
```

profile of v0, /device:TPU:1, one launch (start us, length us, event | category | flops | bytes accessed | tf_op | source)
XLA Modules:
  0.0 618.9 jit_solution(13454673228477233298)
XLA Ops:
  8.2 1.5 copy.30
  15.4 34.2 %psum.21 = f32[48]{0:T(128)S(1)} all-reduce(f32[48]{0:T(128)S(1)} %fusion.7), channel_id=1, replica_groups=mesh['dp'=2,'row'=16,'col'=8] {'row'}, use_global_device_ids=true, to_apply=%region_1.0 | all-reduce | flops 48 | bytes 384 | tf_op jit(solution)/shard_map/psum | solution.py:22
  50.3 22.6 %all_gather.24 = bf16[384,512]{1,0:T(8,128)(2,1)S(1)} all-gather(bf16[48,512]{1,0:T(8,128)(2,1)S(1)} %fusion.2), channel_id=1, replica_groups=mesh['dp'=2,'row'=16,'col'=8] {'col'}, dimensions={0}, use_global_device_ids=true | all-gather | bytes 442368 | tf_op jit(solution)/shard_map/all_gather | solution.py:33
  72.9 2.4 fusion.14
  75.3 2.4 fusion.15
  77.7 3.2 pad_maximum_fusion
  81.7 19.5 %all_gather.29 = bf16[384,512]{1,0:T(8,128)(2,1)S(1)} all-gather(bf16[48,512]{1,0:T(8,128)(2,1)S(1)} %copy-done.10), channel_id=1, replica_groups=mesh['dp'=2,'row'=16,'col'=8] {'col'}, dimensions={0}, use_global_device_ids=true | all-gather | bytes 442368 | tf_op jit(solution)/shard_map/all_gather | solution.py:34
  101.3 2.6 convolution_bitcast_fusion
  103.9 2.3 copy.34
  108.1 105.8 %all-reduce.4.cloned.1.call-done = f32[384,3584]{1,0:T(8,128)} async-done(((f32[384,3584]{1,0:T(8,128)}), f32[384,3584]{1,0:T(8,128)}) %all-reduce.4.cloned.1.call-update) | async-done | bytes 5505040
  213.9 83.0 %reduce-scatter.19.cloned.1.call-done = f32[24,1792]{1,0:T(8,128)} async-done(((f32[384,1792]{1,0:T(8,128)}), f32[24,1792]{1,0:T(8,128)}) %reduce-scatter.19.cloned.1.call-update) | async-done | bytes 172048
  297.0 1.9 multiply_convert_fusion
  300.4 46.9 %all-gather.11.cloned.1.call-done = bf16[384,1792]{1,0:T(8,128)(2,1)} async-done(((bf16[24,1792]{1,0:T(8,128)(2,1)}), bf16[384,1792]{1,0:T(8,128)(2,1)}) %all-gather.11.cloned.1.call-update) | async-done | bytes 1376272 | tf_op jit(solution)/shard_map/all_gather | solution.py:53
  347.3 3.1 fusion.16
  350.5 47.7 %all-gather.15.cloned.1.call-done = bf16[384,1792]{1,0:T(8,128)(2,1)} async-done(((bf16[24,1792]{1,0:T(8,128)(2,1)}), bf16[384,1792]{1,0:T(8,128)(2,1)}) %all-gather.15.cloned.1.call-update) | async-done | bytes 1376272 | tf_op jit(solution)/shard_map/all_gather | solution.py:75
  398.2 2.8 fusion.17
  401.0 48.1 %all-gather.17.cloned.1.call-done = bf16[384,1792]{1,0:T(8,128)(2,1)} async-done(((bf16[24,1792]{1,0:T(8,128)(2,1)}), bf16[384,1792]{1,0:T(8,128)(2,1)}) %all-gather.17.cloned.1.call-update) | async-done | bytes 1376272 | tf_op jit(solution)/shard_map/all_gather | solution.py:76
  449.1 3.1 convolution_add_fusion
  452.3 4.3 fusion.18
  457.9 3.0 fusion.19
  462.2 3.1 fusion.20
  465.7 1.7 copy.36
  467.8 1.7 copy.38
  469.6 17.5 %reduce-scatter.9.cloned.1.call-done = f32[48,512]{1,0:T(8,128)} async-done(((f32[384,512]{1,0:T(8,128)}), f32[48,512]{1,0:T(8,128)}) %reduce-scatter.9.cloned.1.call-update) | async-done | bytes 98320 | tf_op jit(solution)/shard_map/reduce_scatter | solution.py:55
  487.1 1.5 convert_element_type.96
  488.6 37.9 %reduce-scatter.11.cloned.1.call-done = f32[48,512]{1,0:T(8,128)} async-done(((f32[384,512]{1,0:T(8,128)}), f32[48,512]{1,0:T(8,128)}) %reduce-scatter.11.cloned.1.call-update) | async-done | bytes 98320 | tf_op jit(solution)/shard_map/reduce_scatter | solution.py:78
  527.5 33.1 %psum.22 = f32[48]{0:T(128)S(1)} all-reduce(f32[48]{0:T(128)S(1)} %get-tuple-element.7), channel_id=1, replica_groups=mesh['dp'=2,'row'=16,'col'=8] {'row'}, use_global_device_ids=true, to_apply=%region_7.0 | all-reduce | flops 48 | bytes 384 | tf_op jit(solution)/shard_map/psum | solution.py:103
  560.6 40.5 %psum.23 = f32[512]{0:T(512)} all-reduce(f32[512]{0:T(512)S(1)} %get-tuple-element.6), channel_id=1, replica_groups=mesh['dp'=2,'row'=16,'col'=8] {'dp','col'}, use_global_device_ids=true, to_apply=%region_9.0 | all-reduce | flops 512 | bytes 4096 | tf_op jit(solution)/shard_map/psum | solution.py:102
  601.1 1.6 fusion.6
  602.7 3.6 mul.141
  606.3 2.9 mul.142
  610.8 1.6 bitcast_multiply_fusion
  (98 shorter events, 17.1 us)
Async XLA Ops:
  7.2 65.7 %all-gather.7.cloned.1.call-start = ((), (), s32[]{:S(2)}) async-start(), calls=%async_computation.6 | async-start | bytes 2752512 | tf_op jit(solution)/shard_map/all_gather | solution.py:29
  9.6 1.1 copy-start.14
  9.6 1.5 copy-start.6
  10.7 64.7 %all-gather.9.cloned.1.call-start = ((), (), s32[]{:S(2)}) async-start(), calls=%async_computation.7 | async-start | bytes 2752512 | tf_op jit(solution)/shard_map/all_gather | solution.py:30
  11.7 1.1 copy-start.15
  11.7 2.4 copy-start.7
  12.7 88.6 %all-gather.13.cloned.1.call-start = ((), (), s32[]{:S(2)}) async-start(), calls=%async_computation.9 | async-start | bytes 2752512 | tf_op jit(solution)/shard_map/all_gather | solution.py:32
  14.1 1.2 copy-start.8
  14.1 36.1 %copy-start.11 = (f32[512]{0:T(512)S(1)}, f32[512]{0:T(512)}, u32[]{:S(2)}) copy-start(f32[512]{0:T(512)} %param.10) | copy-start | bytes 6148
  15.2 198.7 %all-reduce.4.cloned.1.call-start = ((), (), s32[]{:S(2)}) async-start(), calls=%async_computation.17 | async-start | bytes 11010048
  49.6 0.6 copy-start.12
  80.9 0.8 copy-start.10
  81.0 216.0 %reduce-scatter.19.cloned.1.call-start = ((), (), s32[]{:S(2)}) async-start(), calls=%async_computation.18 | async-start | bytes 2924544
  106.2 0.7 copy-start.16
  106.2 241.1 %copy-start.1 = (bf16[1792,512]{1,0:T(8,128)(2,1)S(1)}, bf16[1792,512]{1,0:T(8,128)(2,1)}, u32[]{:S(2)}) copy-start(bf16[1792,512]{1,0:T(8,128)(2,1)} %all-gather.13.cloned.1.call-done) | copy-start | bytes 5505028
  106.2 241.1 %all-gather.11.cloned.1.call-start = ((), (), s32[]{:S(2)}) async-start(), calls=%async_computation.8 | async-start | bytes 1462272 | tf_op jit(solution)/shard_map/all_gather | solution.py:53
  298.9 99.3 %all-gather.15.cloned.1.call-start = ((), (), s32[]{:S(2)}) async-start(), calls=%async_computation.11 | async-start | bytes 1462272 | tf_op jit(solution)/shard_map/all_gather | solution.py:75
  299.6 149.4 %all-gather.17.cloned.1.call-start = ((), (), s32[]{:S(2)}) async-start(), calls=%async_computation.12 | async-start | bytes 1462272 | tf_op jit(solution)/shard_map/all_gather | solution.py:76
  300.4 186.7 %reduce-scatter.9.cloned.1.call-start = ((), (), s32[]{:S(2)}) async-start(), calls=%async_computation.10 | async-start | bytes 884736 | tf_op jit(solution)/shard_map/reduce_scatter | solution.py:55
  350.5 98.6 %copy-start.3 = (bf16[512,1792]{0,1:T(8,128)(2,1)S(1)}, bf16[512,1792]{0,1:T(8,128)(2,1)}, u32[]{:S(2)}) copy-start(bf16[512,1792]{0,1:T(8,128)(2,1)} %all-gather.9.cloned.1.call-done) | copy-start | bytes 5505028
  350.5 176.0 %reduce-scatter.11.cloned.1.call-start = ((), (), s32[]{:S(2)}) async-start(), calls=%async_computation.13 | async-start | bytes 884736 | tf_op jit(solution)/shard_map/reduce_scatter | solution.py:78
  452.2 150.5 %reduce-scatter.13.cloned.1.call-start = ((), (), s32[]{:S(2)}) async-start(), calls=%async_computation.14 | async-start | bytes 5505024 | tf_op jit(solution)/shard_map/reduce_scatter | solution.py:95
  456.5 1.3 copy-start.5
  456.6 149.8 %reduce-scatter.15.cloned.1.call-start = ((), (), s32[]{:S(2)}) async-start(), calls=%async_computation.15 | async-start | bytes 5505024 | tf_op jit(solution)/shard_map/reduce_scatter | solution.py:96
  460.9 1.3 copy-start.2
  460.9 148.4 %reduce-scatter.17.cloned.1.call-start = ((), (), s32[]{:S(2)}) async-start(), calls=%async_computation.16 | async-start | bytes 5505024 | tf_op jit(solution)/shard_map/reduce_scatter | solution.py:98
  467.8 58.7 %copy-start.9 = (bf16[48,512]{1,0:T(8,128)(2,1)S(1)}, bf16[48,512]{1,0:T(8,128)(2,1)}, u32[]{:S(2)}) copy-start(bf16[48,512]{1,0:T(8,128)(2,1)} %param.9) | copy-start | bytes 147460
  467.8 58.7 %copy-start.13 = (f32[48]{0:T(128)S(1)}, f32[48]{0:T(128)}, u32[]{:S(2)}) copy-start(f32[48]{0:T(128)} %copy-done.12) | copy-start | bytes 580
  602.7 3.6 copy-start
  609.3 1.5 copy-start.4
Sparse Core Ops, SparseCore 0:
  10.8 20.0 all-gather.6
  33.2 16.8 all-gather.8
  52.5 16.8 all-gather.12
  81.1 132.8 all-reduce.3
  217.4 79.5 reduce-scatter.18
  299.9 47.4 all-gather.10
  350.4 47.7 all-gather.14
  401.3 47.7 all-gather.16
  452.2 34.8 reduce-scatter.8
  489.5 36.9 reduce-scatter.10
  529.0 20.7 reduce-scatter.12
  552.1 18.3 reduce-scatter.14
  573.0 18.6 reduce-scatter.16
where the time goes:
time: 620 us; the launch traced here: 619 us
  waiting for transfers between devices  388 us (63%)
  blocking collectives  150 us (24%)
  matrix products  26.8 us (4%)
  other arithmetic  21.5 us (3%)
  local copies, waits for them, and re-layouts  17 us (3%)
  between operations  14.8 us (2%)
    unnamed x15, waiting for transfers between devices  190 us
    all_gather x1, waiting for transfers between devices, on_device(): lax.all_gather(up_grad, 'row', axis=0, tiled=True)  48.1 us
    all_gather x1, waiting for transfers between devices, on_device(): lax.all_gather(gate_grad, 'row', axis=0, tiled=True)  47.7 us
    all_gather x1, waiting for transfers between devices, on_device(): lax.all_gather(activate(gate_part, up_part), 'row', axis=0, tiled=True)  46.9 us
    psum x1, blocking collectives, on_device(): lax.psum(jnp.sum(normed_grad * token_f * inv_rms, axis=0), ('dp', 'col'))  40.5 us
    reduce_scatter x1, waiting for transfers between devices, on_device(): lax.psum_scatter(lax.dot_general(gate_grads, gate_full, contract_last, pr...  37.9 us
    psum x1, blocking collectives, on_device(): square = lax.psum(jnp.sum(token_f * token_f, axis=1), 'row')  34.2 us
    psum x1, blocking collectives, on_device(): lax.psum(jnp.sum(norm_gain * normed_grad * token_f, axis=1), 'row')  33.1 us
  transfers between devices with their start and end apart: 13, of which 7 were waited for; matrix products, arithmetic and copies ran while one was open for 8% of the time, Pallas kernels for 0%

commit v1 on v0

v1 whole, which is shorter than its diff:
```python
import jax
import jax.numpy as jnp
from jax import lax
from jax.experimental import pallas as pl
from jax.experimental.pallas import tpu as pltpu
from jax.sharding import PartitionSpec as P

D = 8192
BLOCK = 128
T = 48
W = 512
U = 896
F32 = jnp.float32
BF16 = jnp.bfloat16
MESH = pl.DeviceIdType.MESH
VM = pl.BlockSpec(memory_space=pltpu.VMEM)
VMEM_LIMIT = 48 * 1024 * 1024


def rcopy(src, dst, send, recv, dev):
    return pltpu.make_async_remote_copy(
        src_ref=src, dst_ref=dst, send_sem=send, recv_sem=recv, device_id=dev, device_id_type=MESH
    )


def greet(devices):
    barrier = pltpu.get_barrier_semaphore()
    for dev in devices:
        pl.semaphore_signal(barrier, inc=1, device_id=dev, device_id_type=MESH)
    pl.semaphore_wait(barrier, len(devices))


def add(*values):
    total = values[0].astype(F32)
    for value in values[1:]:
        total = total + value.astype(F32)
    return total


def peers_of_row(row):
    return [{"row": lax.rem(row + k, 16)} for k in range(1, 16)]


def peers_of_cols(dp, z):
    me = dp * 8 + z
    found = []
    for k in range(1, 16):
        other = lax.rem(me + k, 16)
        found.append({"dp": other // 8, "col": lax.rem(other, 8)})
    return found


def gather_kernel(
    tok, cot, squares, x_out, c_out, inv_out, sq_buf,
    ring_send, ring_recv, pair_send, pair_recv, sq_send, sq_recv, inv_send, inv_recv,
):
    dp, row, z = lax.axis_index("dp"), lax.axis_index("row"), lax.axis_index("col")
    row_peers = peers_of_row(row)
    col_peers = peers_of_cols(dp, z)
    right, left = {"col": lax.rem(z + 1, 8)}, {"col": lax.rem(z + 7, 8)}
    mate = {"dp": 1 - dp}
    x_out[dp, z] = tok[...]
    c_out[dp, z] = cot[...]
    sq_buf[row] = squares[...]
    greet(row_peers + col_peers)
    outs = (x_out, c_out)
    started = []

    def begin(copy):
        copy.start()
        started.append(copy)
        return copy

    squared = [
        begin(rcopy(squares, sq_buf.at[row], sq_send.at[k], sq_recv.at[k], row_peers[k]))
        for k in range(15)
    ]

    def ring(side, step, unit):
        block = lax.rem(z + (9 - step if side == 0 else step + 7), 8)
        here = (tok, cot)[unit] if step == 1 else outs[unit].at[dp, block]
        return begin(
            rcopy(
                here, outs[unit].at[dp, block],
                ring_send.at[side, step - 1, unit], ring_recv.at[side, step - 1, unit],
                right if side == 0 else left,
            )
        )

    def pair(slot, block, unit, own=False):
        here = (tok, cot)[unit] if own else outs[unit].at[dp, block]
        begin(rcopy(here, outs[unit].at[dp, block], pair_send.at[slot, unit], pair_recv.at[slot, unit], mate))

    flying = {}
    for unit in range(2):
        for side in range(2):
            u = unit if side == 0 else 1 - unit
            flying[side, 1, u] = ring(side, 1, u)
    for unit in range(2):
        pair(0, z, unit, own=True)

    inv_done = []
    for step in range(1, 5):
        for unit in range(2):
            for side in range(2):
                u = unit if side == 0 else 1 - unit
                if step == 4 and u != side:
                    continue
                flying[side, step, u].wait_recv()
                if step < 3 or (step == 3 and u == side):
                    flying[side, step + 1, u] = ring(side, step + 1, u)
                block = lax.rem(z + (8 - step if side == 0 else step), 8)
                slot = step if side == 0 or step == 4 else step + 4
                pair(slot, block, u)
        if step == 1:
            for copy in squared:
                copy.wait_recv()
            total = sq_buf[0]
            for k in range(1, 16):
                total = total + sq_buf[k]
            inv_out[dp * 8 + z] = lax.rsqrt(total / D + 1e-05)
            inv_done = [
                begin(
                    rcopy(
                        inv_out.at[dp * 8 + z], inv_out.at[dp * 8 + z],
                        inv_send.at[k], inv_recv.at[k], col_peers[k],
                    )
                )
                for k in range(15)
            ]
    for slot in range(8):
        for unit in range(2):
            rcopy(
                tok, x_out.at[1 - dp, z], pair_send.at[slot, unit], pair_recv.at[slot, unit], mate
            ).wait_recv()
    for copy in inv_done:
        copy.wait_recv()
    for copy in started:
        copy.wait_send()


def gather(tok, cot, squares):
    return pl.pallas_call(
        gather_kernel,
        out_shape=(
            jax.ShapeDtypeStruct((2, 8, T, W), BF16),
            jax.ShapeDtypeStruct((2, 8, T, W), BF16),
            jax.ShapeDtypeStruct((16, 1, 128), F32),
        ),
        in_specs=[VM] * 3,
        out_specs=(VM,) * 3,
        scratch_shapes=[
            pltpu.VMEM((16, 1, 128), F32),
            pltpu.SemaphoreType.DMA((2, 4, 2)),
            pltpu.SemaphoreType.DMA((2, 4, 2)),
            pltpu.SemaphoreType.DMA((8, 2)),
            pltpu.SemaphoreType.DMA((8, 2)),
            pltpu.SemaphoreType.DMA((15,)),
            pltpu.SemaphoreType.DMA((15,)),
            pltpu.SemaphoreType.DMA((15,)),
            pltpu.SemaphoreType.DMA((15,)),
        ],
        compiler_params=pltpu.CompilerParams(
            collective_id=0, has_side_effects=True, vmem_limit_bytes=VMEM_LIMIT
        ),
        name="gather_tokens",
    )(tok, cot, squares)


LANES = 3 * U
PARTS = (((0, 768), (768, 640)), ((1408, 640), (2048, 640)))


class Ring:
    def __init__(self, pos, right, left):
        self.here = pos
        self.next = lax.rem(pos + 1, 4)
        self.far = lax.rem(pos + 2, 4)
        self.prev = lax.rem(pos + 3, 4)
        self.right, self.left = right, left


class Scatter:
    def __init__(self, ring, src, bufs, send, recv, started):
        self.ring, self.src, self.bufs = ring, src, bufs
        self.send, self.recv, self.started = send, recv, started
        self.copies = {}

    def go(self, k, src, dst, dev):
        copy = rcopy(src, dst, self.send.at[k], self.recv.at[k], dev)
        copy.start()
        self.started.append(copy)
        self.copies[k] = copy

    def begin(self):
        ring, src, b = self.ring, self.src, self.bufs
        self.go(0, src(ring.far, 0), b["hop"][0], ring.right)
        self.go(1, src(ring.far, 1), b["hop"][1], ring.left)
        self.go(2, src(ring.next, 1), b["left"][1], ring.right)
        self.go(3, src(ring.prev, 0), b["right"][0], ring.left)

    def middle(self, part):
        ring, src, b = self.ring, self.src, self.bufs
        self.copies[part].wait_recv()
        piece = src(ring.next if part == 0 else ring.prev, part)
        b["sum"][part][...] = add(piece[...], b["hop"][part][...]).astype(BF16)
        if part == 0:
            self.go(4, b["sum"][0], b["left"][0], ring.right)
        else:
            self.go(5, b["sum"][1], b["right"][1], ring.left)

    def end(self, part):
        b = self.bufs
        for k in ((3, 4), (2, 5))[part]:
            self.copies[k].wait_recv()
        own = self.src(self.ring.here, part)
        return add(own[...], b["left"][part][...], b["right"][part][...])


class Spread:
    def __init__(self, ring, slot, send, recv, started):
        self.ring, self.slot = ring, slot
        self.send, self.recv, self.started = send, recv, started
        self.copies = {}

    def go(self, k, ref, dev):
        copy = rcopy(ref, ref, self.send.at[k], self.recv.at[k], dev)
        copy.start()
        self.started.append(copy)
        self.copies[k] = copy

    def begin(self):
        ring, slot = self.ring, self.slot
        self.go(0, slot(ring.here, 0), ring.right)
        self.go(1, slot(ring.here, 1), ring.left)
        self.go(2, slot(ring.here, 1), ring.right)
        self.go(3, slot(ring.here, 0), ring.left)

    def middle(self, part):
        ring, slot = self.ring, self.slot
        self.copies[part].wait_recv()
        if part == 0:
            self.go(4, slot(ring.prev, 0), ring.right)
        else:
            self.go(5, slot(ring.next, 1), ring.left)

    def end(self):
        for k in range(2, 6):
            self.copies[k].wait_recv()


def activation(gate, up_value, hidden_grad):
    s = jax.nn.sigmoid(gate)
    hidden = (gate * s * up_value).astype(BF16)
    gate_grad = (hidden_grad * up_value * s * (1.0 + gate * (1.0 - s))).astype(BF16)
    up_grad = (hidden_grad * gate * s).astype(BF16)
    return hidden, gate_grad, up_grad


def exchange_kernel(p, q, *scratch):
    n = 0

    def take(count):
        nonlocal n
        n += count
        return scratch[n - count : n]

    big, small = [], []
    for store in (big, small):
        for chain in range(2):
            store.append({name: take(2) for name in ("hop", "sum", "left", "right")})
    mid = [take(2), take(2)]
    (total,) = take(1)
    send, recv = take(2)
    row = lax.axis_index("row")
    px, py = row // 4, lax.rem(row, 4)

    def at(x, y):
        return {"row": x * 4 + y}

    rings = (
        Ring(px, at(lax.rem(px + 1, 4), py), at(lax.rem(px + 3, 4), py)),
        Ring(py, at(px, lax.rem(py + 1, 4)), at(px, lax.rem(py + 3, 4))),
    )
    greet([rings[0].right, rings[0].left, rings[1].right, rings[1].left])
    started = []

    def lanes(chain, part):
        start, size = PARTS[chain][part]
        return pl.ds(start, size)

    def first_piece(ref, chain):
        if chain == 0:
            return lambda d, part: ref.at[d, :, :, lanes(chain, part)]
        return lambda d, part: ref.at[:, d, :, lanes(chain, part)]

    stage1 = [
        Scatter(rings[c], first_piece(p, c), big[c], send.at[c, 0], recv.at[c, 0], started) for c in range(2)
    ]
    for part in range(1):
        for c in range(2):
            stage1[c].begin()
    for part in range(2):
        for c in range(2):
            stage1[c].middle(part)
    stage2 = []
    for c in range(2):
        for part in range(2):
            mid[c][part][...] = stage1[c].end(part).astype(BF16)
        stage2.append(
            Scatter(
                rings[1 - c], lambda d, part, c=c: mid[c][part].at[d], small[c],
                send.at[c, 1], recv.at[c, 1], started,
            )
        )
        stage2[c].begin()
    for c in range(2):
        for part in range(2):
            stage2[c].middle(part)
    for c in range(2):
        for part in range(2):
            total[:, lanes(c, part)] = stage2[c].end(part)
    hidden, gate_grad, up_grad = activation(
        total[:, pl.ds(0, U)], total[:, pl.ds(U, U)], total[:, pl.ds(2 * U, U)]
    )
    q[px, py, :, pl.ds(0, U)] = hidden
    q[px, py, :, pl.ds(U, U)] = gate_grad
    q[px, py, :, pl.ds(2 * U, U)] = up_grad

    def near(c):
        if c == 0:
            return lambda d, part: q.at[px, d, :, lanes(c, part)]
        return lambda d, part: q.at[d, py, :, lanes(c, part)]

    stage3 = [Spread(rings[1 - c], near(c), send.at[c, 2], recv.at[c, 2], started) for c in range(2)]
    stage4 = [Spread(rings[c], first_piece(q, c), send.at[c, 3], recv.at[c, 3], started) for c in range(2)]
    for c in range(2):
        stage3[c].begin()
    for part in range(2):
        for c in range(2):
            stage3[c].middle(part)
    for c in range(2):
        stage3[c].end()
        stage4[c].begin()
    for part in range(2):
        for c in range(2):
            stage4[c].middle(part)
    for c in range(2):
        stage4[c].end()
    for copy in started:
        copy.wait_send()


def exchange(partials):
    scratch = []
    for lead in ((4, T), (T,)):
        for chain in range(2):
            for _ in range(4):
                for part in range(2):
                    scratch.append(pltpu.VMEM(lead + (PARTS[chain][part][1],), BF16))
    for chain in range(2):
        for part in range(2):
            scratch.append(pltpu.VMEM((4, T, PARTS[chain][part][1]), BF16))
    scratch.append(pltpu.VMEM((T, LANES), F32))
    scratch += [pltpu.SemaphoreType.DMA((2, 4, 6))] * 2
    return pl.pallas_call(
        exchange_kernel,
        out_shape=jax.ShapeDtypeStruct((4, 4, T, LANES), BF16),
        in_specs=[VM],
        out_specs=VM,
        scratch_shapes=scratch,
        compiler_params=pltpu.CompilerParams(
            collective_id=1, has_side_effects=True, vmem_limit_bytes=VMEM_LIMIT
        ),
        name="exchange_hidden",
    )(partials)


def finish_kernel(
    branch_part, grad_part, tok, inv, gain, branch_out, tokens_out, gain_out,
    pair_buf, go_buf, come_buf, square_buf, dot_buf, gain_buf,
    pair_send, pair_recv, ring_send, ring_recv, dot_send, dot_recv, gain_send, gain_recv,
):
    dp, row, z = lax.axis_index("dp"), lax.axis_index("row"), lax.axis_index("col")
    row_peers = peers_of_row(row)
    col_peers = peers_of_cols(dp, z)
    right, left = {"col": lax.rem(z + 1, 8)}, {"col": lax.rem(z + 7, 8)}
    mate = {"dp": 1 - dp}
    parts = (branch_part, grad_part)
    greet(row_peers + col_peers)
    started = []

    def begin(copy):
        copy.start()
        started.append(copy)
        return copy

    offsets = (4, 3, 5, 2, 6, 1, 7, 0)
    paired = {}
    for off in offsets:
        dest = lax.rem(z + off, 8)
        for unit in range(2):
            paired[off, unit] = begin(
                rcopy(
                    parts[unit].at[1 - dp, dest], pair_buf.at[unit, off],
                    pair_send.at[unit, off], pair_recv.at[unit, off], mate,
                )
            )
    known = set()

    def mine(off, unit):
        if (off, unit) not in known:
            paired[off, unit].wait_recv()
            known.add((off, unit))
        return add(parts[unit][dp, lax.rem(z + off, 8)], pair_buf[unit, off])

    ring = {}
    for step in range(1, 5):
        for unit in range(2):
            for side in range(2):
                u = unit if side == 0 else 1 - unit
                if step == 1 and u != side:
                    continue
                off = 5 - step if side == 0 else 3 + step
                value = mine(off, u)
                if step > 2 or (step == 2 and u == side):
                    ring[side, step - 1, u].wait_recv()
                    value = value + come_buf[side, step - 2, u].astype(F32)
                go_buf[side, step - 1, u] = value.astype(BF16)
                ring[side, step, u] = begin(
                    rcopy(
                        go_buf.at[side, step - 1, u], come_buf.at[side, step - 1, u],
                        ring_send.at[side, step - 1, u], ring_recv.at[side, step - 1, u],
                        right if side == 0 else left,
                    )
                )
    totals = []
    for unit in range(2):
        value = mine(0, unit)
        for side in range(2):
            ring[side, 4, unit].wait_recv()
            value = value + come_buf[side, 3, unit].astype(F32)
        totals.append(value)
    branch_out[...] = totals[0].astype(BF16)
    normed_grad = totals[1]
    token_f = tok[...].astype(F32)
    inv_rms = inv[:, 0:1]
    weighted = normed_grad * token_f
    gain_buf[dp * 8 + z] = jnp.sum(weighted * inv_rms, axis=0, keepdims=True)
    square_buf[...] = jnp.zeros((128, 128), F32)
    square_buf[pl.ds(0, T), :] = jnp.broadcast_to(
        jnp.sum(gain[...] * weighted, axis=1, keepdims=True), (T, 128)
    )
    dot_buf[row] = jnp.transpose(square_buf[...])[0:1]
    small = []
    for k in range(15):
        small.append(
            begin(rcopy(dot_buf.at[row], dot_buf.at[row], dot_send.at[k], dot_recv.at[k], row_peers[k]))
        )
        mine_at = gain_buf.at[dp * 8 + z]
        small.append(begin(rcopy(mine_at, mine_at, gain_send.at[k], gain_recv.at[k], col_peers[k])))
    for copy in small:
        copy.wait_recv()
    inner, gain_total = dot_buf[0], gain_buf[0]
    for k in range(1, 16):
        inner = inner + dot_buf[k]
        gain_total = gain_total + gain_buf[k]
    gain_out[...] = gain_total
    square_buf[...] = jnp.transpose(jnp.broadcast_to(inner, (128, 128)))
    inner_col = square_buf[pl.ds(0, T), 0:1]
    tokens_out[...] = inv_rms * gain[...] * normed_grad - token_f * inv_rms * inv_rms * inv_rms * inner_col / D
    for copy in started:
        copy.wait_send()


def finish(branch_part, grad_part, tok, inv, gain):
    return pl.pallas_call(
        finish_kernel,
        out_shape=(
            jax.ShapeDtypeStruct((T, W), BF16),
            jax.ShapeDtypeStruct((T, W), F32),
            jax.ShapeDtypeStruct((1, W), F32),
        ),
        in_specs=[VM] * 5,
        out_specs=(VM,) * 3,
        scratch_shapes=[
            pltpu.VMEM((2, 8, T, W), BF16),
            pltpu.VMEM((2, 4, 2, T, W), BF16),
            pltpu.VMEM((2, 4, 2, T, W), BF16),
            pltpu.VMEM((128, 128), F32),
            pltpu.VMEM((16, 1, 128), F32),
            pltpu.VMEM((16, 1, W), F32),
            pltpu.SemaphoreType.DMA((2, 8)),
            pltpu.SemaphoreType.DMA((2, 8)),
            pltpu.SemaphoreType.DMA((2, 4, 2)),
            pltpu.SemaphoreType.DMA((2, 4, 2)),
            pltpu.SemaphoreType.DMA((15,)),
            pltpu.SemaphoreType.DMA((15,)),
            pltpu.SemaphoreType.DMA((15,)),
            pltpu.SemaphoreType.DMA((15,)),
        ],
        compiler_params=pltpu.CompilerParams(
            collective_id=2, has_side_effects=True, vmem_limit_bytes=VMEM_LIMIT
        ),
        name="finish_tokens",
    )(branch_part, grad_part, tok, inv, gain)


def expand_keep(keep, target_type):
    return jnp.repeat(jnp.repeat(keep, BLOCK, axis=0), BLOCK, axis=1).astype(target_type)


LAST = (((1,), (1,)), ((), ()))
FIRST = (((0,), (0,)), ((), ()))


def on_device(
    tokens, norm_gain, gate_weight, up_weight, down_weight, gate_keep, up_keep, down_keep, cotangent
):
    gain = norm_gain[None, :]
    token_f = tokens.astype(F32)
    squares = jnp.pad(jnp.sum(token_f * token_f, axis=1), (0, 128 - T))[None, :]
    seen, cot, inv = gather(tokens, cotangent, squares)
    seen, cot = seen.reshape(16 * T, W), cot.reshape(16 * T, W)
    inv_all = inv[:, 0, :T].reshape(16 * T, 1)
    normed = (seen.astype(F32) * inv_all * gain).astype(BF16)
    keep_gu = jnp.concatenate([expand_keep(gate_keep, BF16), expand_keep(up_keep, BF16)], axis=1)
    gu_masked = jnp.concatenate([gate_weight, up_weight], axis=1) * keep_gu
    down_masked = down_weight * expand_keep(down_keep, BF16)
    gate_up = jnp.dot(normed, gu_masked, preferred_element_type=F32).astype(BF16)
    hidden_grad = lax.dot_general(cot, down_masked, LAST, preferred_element_type=F32).astype(BF16)
    partials = jnp.concatenate([gate_up, hidden_grad], axis=1).reshape(4, 4, T, LANES)
    shared = exchange(partials).reshape(16 * T, LANES)
    hidden, gu_grad = shared[:, :U], shared[:, U:]
    branch_part = jnp.dot(hidden, down_masked, preferred_element_type=F32).astype(BF16)
    grad_part = lax.dot_general(gu_grad, gu_masked, LAST, preferred_element_type=F32).astype(BF16)
    index = lax.axis_index("dp") * 8 + lax.axis_index("col")
    inv_own = jnp.broadcast_to(inv[index, 0, :T][:, None], (T, 128))
    branch, grad_tokens, grad_gain = finish(
        branch_part.reshape(2, 8, T, W), grad_part.reshape(2, 8, T, W), tokens, inv_own, gain
    )
    grad_gate = lax.dot_general(normed, gu_grad[:, :U], FIRST, preferred_element_type=F32)
    grad_up = lax.dot_general(normed, gu_grad[:, U:], FIRST, preferred_element_type=F32)
    grad_down = lax.dot_general(hidden, cot, FIRST, preferred_element_type=F32)
    return (
        branch,
        grad_tokens,
        grad_gain[0],
        grad_gate * expand_keep(gate_keep, F32),
        grad_up * expand_keep(up_keep, F32),
        grad_down * expand_keep(down_keep, F32),
    )


def solution(mesh):
    wide = P("row", ("dp", "col"))
    tall = P(("dp", "col"), "row")
    return jax.shard_map(
        on_device,
        mesh=mesh,
        in_specs=(tall, P("row"), wide, wide, tall, wide, wide, tall, tall),
        out_specs=(tall, tall, P("row"), wide, wide, tall),
        check_vma=False,
    )
```

time: 620 us -> 155 us (0.25)
  waiting for transfers between devices: 388 us -> 0 us
  blocking collectives: 150 us -> 0 us
  Pallas kernels: 0 us -> 111 us
  other arithmetic: 21.5 us -> 4.84 us
  between operations: 14.8 us -> 0.86 us
    unnamed x15 -> x0, waiting for transfers between devices: 190 us -> none
    all_gather x6 -> x0, waiting for transfers between devices: 143 us -> none  [the longest x1 48.1 us: on_device(): lax.all_gather(up_grad, 'row', axis=0, tiled=True)]
    pallas_call x0 -> x3, Pallas kernels: none -> 111 us  [the longest x1 53.1 us: exchange(): pl.pallas_call(exchange_kernel, out_shape=jax.ShapeDtypeStruct((4, 4, T,...]
    psum x3 -> x0, blocking collectives: 108 us -> none  [the longest x1 40.5 us: on_device(): lax.psum(jnp.sum(normed_grad * token_f * inv_rms, axis=0), ('dp', 'col'))]
    reduce_scatter x5 -> x0, waiting for transfers between devices: 55.3 us -> none  [the longest x1 37.9 us: on_device(): lax.psum_scatter(lax.dot_general(gate_grads, gate_full, contract_last, pr...]
    all_gather x2 -> x0, blocking collectives: 42.1 us -> none  [the longest x1 22.6 us: on_device(): seen_rows = lax.all_gather(normed, 'col', axis=0, tiled=True)]
    mul x6 -> x0, other arithmetic: 11.2 us -> none  [the longest x1 3.6 us: on_device(): grad_gate = gate_total * expand_keep(gate_keep, jnp.float32)]
    dot_general x9 -> x7, matrix products: 26.8 us -> 22.2 us  [the longest x1 4.94 us: on_device(): jnp.dot(normed, gu_masked, preferred_element_type=F32).astype(BF16)]
  transfers between devices with their start and end apart: 13 -> 0, of which waited for: 7 -> 0; matrix products, arithmetic and copies ran while one was open for 8% -> 0% of each run, Pallas kernels for 0% -> 0%
where the time goes in v1:
time: 155 us
  Pallas kernels  111 us (72%)
  matrix products  22.2 us (14%)
  local copies, waits for them, and re-layouts  16.5 us (11%)
  other arithmetic  4.84 us (3%)
    pallas_call x1, Pallas kernels, exchange(): pl.pallas_call(exchange_kernel, out_shape=jax.ShapeDtypeStruct((4, 4, T,...  53.1 us
    pallas_call x1, Pallas kernels, finish(): pl.pallas_call(finish_kernel, out_shape=(jax.ShapeDtypeStruct((T, W), BF1...  30.2 us
    pallas_call x1, Pallas kernels, gather(): pl.pallas_call(gather_kernel, out_shape=(jax.ShapeDtypeStruct((2, 8, T, W...  27.3 us
    unnamed x43, local copies, waits for them, and re-layouts  7.63 us
    dot_general x1, matrix products, on_device(): jnp.dot(normed, gu_masked, preferred_element_type=F32).astype(BF16)  4.94 us
    broadcast_in_dim x6, local copies, waits for them, and re-layouts, expand_keep(): jnp.repeat(jnp.repeat(keep, BLOCK, axis=0), BLOCK, axis=1)  4.67 us
    dot_general x1, matrix products, on_device(): lax.dot_general(normed, gu_grad[:, U:], FIRST, preferred_element_type=F32)  4.39 us
    dot_general x1, matrix products, on_device(): lax.dot_general(normed, gu_grad[:, :U], FIRST, preferred_element_type=F32)  4.39 us

profile of v1, /device:TPU:1, one launch (start us, length us, event | category | flops | bytes accessed | tf_op | source)
XLA Modules:
  0.0 155.0 jit_solution(14149831242828902531)
XLA Ops:
  0.6 0.9 multiply_reduce_fusion
  1.6 0.8 copy-done.1
  2.4 0.8 copy-done.3
  3.2 27.3 %gather_tokens.1 = (bf16[2,8,48,512]{3,2,1,0:T(8,128)(2,1)S(1)}, bf16[2,8,48,512]{3,2,1,0:T(8,128)(2,1)S(1)}, f32[16,1,128]{2,1,0:T(1,128)S(1)}) custom-call(bf16[48,512]{1,0:T(8,128)(2,1)S(1)} %copy-done.1, bf16[48,512]{1,0:T(8,128)(2,1)S(1)} %copy-done.3, f32[1,128]{1,0:T(1,128)S(1)} %pad_bitcast_fusion.squares), custom_call_target="tpu_custom_call" | custom-call | tf_op jit(solution)/shard_map/gather_tokens/pallas_call | solution.py:143
  30.6 0.9 fusion.3
  31.5 0.8 fusion.13
  32.5 1.0 broadcast_in_dim.51
  33.5 0.1 copy.20
  33.7 1.0 broadcast_in_dim.53
  34.7 1.3 copy.17
  36.0 2.3 %copy.18 = bf16[512,896]{0,1:T(8,128)(2,1)} copy(bf16[512,896]{1,0:T(8,128)(2,1)} %param.12) | data formatting | bytes 1835008 | tf_op args[3]
  38.3 4.9 %convolution_convert_fusion = bf16[768,1792]{1,0:T(8,128)(2,1)} fusion(bf16[768,512]{1,0:T(8,128)(2,1)S(1)} %fusion.3, bf16[512,896]{0,1:T(8,128)(2,1)} %copy.18, bf16[512,896]{0,1:T(8,128)(2,1)} %copy.17, bf16[512,896]{0,1:T(8,128)(2,1)} %bitcast.79, bf16[512,896]{0,1:T(8,128)(2,1)S(1)} %bitcast.77), kind=kOutput, calls=%fused_computation.1 | convolution fusion | flops 1418002432 | bytes 7208960 | tf_op jit(solution)/shard_map/dot_general | solution.py:530
  43.2 0.1 copy.21
  43.4 1.1 broadcast_in_dim.55
  44.5 2.4 %convolution_convert_fusion.1 = bf16[768,896]{1,0:T(8,128)(2,1)S(1)} fusion(bf16[768,512]{1,0:T(8,128)(2,1)S(1)} %bitcast.68, bf16[896,512]{1,0:T(8,128)(2,1)} %param.13, bf16[112,8,4,128]{3,2,1,0:T(4,128)(2,1)S(1)} %bitcast.81), kind=kOutput, calls=%fused_computation.6 | convolution fusion | flops 705789952 | bytes 3997696 | tf_op jit(solution)/shard_map/dot_general | solution.py:531
  46.9 2.2 %pad_maximum_fusion = bf16[768,2688]{1,0:T(8,128)(2,1)} fusion(bf16[768,896]{1,0:T(8,128)(2,1)S(1)} %convolution_convert_fusion.1, bf16[768,1792]{1,0:T(8,128)(2,1)S(1)} %copy-done.6), kind=kLoop, calls=%fused_computation | loop fusion | flops 8257536 | bytes 8257536 | tf_op jit(solution)/shard_map/concatenate | solution.py:532
  49.1 53.1 %exchange_hidden.1 = bf16[4,4,48,2688]{3,2,1,0:T(8,128)(2,1)S(1)} custom-call(bf16[4,4,48,2688]{3,2,1,0:T(8,128)(2,1)} %bitcast.72), custom_call_target="tpu_custom_call" | custom-call | tf_op jit(solution)/shard_map/exchange_hidden/pallas_call | solution.py:366
  102.2 1.6 %fusion.4 = bf16[768,512]{1,0:T(8,128)(2,1)S(1)} fusion(bf16[768,2688]{1,0:T(8,128)(2,1)S(1)} %bitcast.61, bf16[512,896]{0,1:T(8,128)(2,1)S(1)} %copy-done.11, bf16[512,896]{0,1:T(8,128)(2,1)S(1)} %copy-done.10, bf16[512,896]{0,1:T(8,128)(2,1)S(1)} %bitcast.80, bf16[512,896]{0,1:T(8,128)(2,1)S(1)} %bitcast.78), kind=kOutput, calls=%fused_computation.12 | convolution fusion | flops 1417019392 | bytes 7208960 | tf_op jit(solution)/shard_map/dot_general | solution.py:536
  103.9 0.2 copy-done
  104.1 1.0 convolution_convert_fusion.2
  105.2 30.2 %finish_tokens.1 = (bf16[48,512]{1,0:T(8,128)(2,1)S(1)}, f32[48,512]{1,0:T(8,128)S(1)}, f32[1,512]{1,0:T(1,128)S(1)}) custom-call(bf16[2,8,48,512]{3,2,1,0:T(8,128)(2,1)S(1)} %bitcast.67, bf16[2,8,48,512]{3,2,1,0:T(8,128)(2,1)S(1)} %bitcast.66, bf16[48,512]{1,0:T(8,128)(2,1)S(1)} %copy-done.2, f32[48,128]{1,0:T(8,128)S(1)} %broadcast_in_dim.57.inv, ...), custom_call_target="tpu_custom_call" | custom-call | tf_op jit(solution)/shard_map/finish_tokens/pallas_call | solution.py:477
  135.6 0.2 broadcast_in_dim.62
  135.9 1.7 %copy.25 = f32[512,896]{1,0:T(8,128)} copy(f32[512,896]{0,1:T(8,128)S(1)} %bitcast.73) | data formatting | bytes 3670016 | tf_op jit(solution)/shard_map/convert_element_type | solution.py:510
  137.6 4.4 %convolution_multiply_fusion = f32[512,896]{1,0:T(8,128)} fusion(f32[512,896]{1,0:T(8,128)} %copy.25, bf16[768,512]{1,0:T(8,128)(2,1)} %copy-done.5, bf16[768,2688]{1,0:T(8,128)(2,1)} %bitcast.63), kind=kOutput, calls=%fused_computation.10 | convolution fusion | flops 705101824 | bytes 5832704 | tf_op jit(solution)/shard_map/dot_general | solution.py:543
  142.1 0.2 broadcast_in_dim.60
  142.4 1.7 %copy.23 = f32[512,896]{1,0:T(8,128)} copy(f32[512,896]{0,1:T(8,128)S(1)} %bitcast.74) | data formatting | bytes 3670016 | tf_op jit(solution)/shard_map/convert_element_type | solution.py:510
  144.0 4.4 %convolution_multiply_fusion.1 = f32[512,896]{1,0:T(8,128)} fusion(f32[512,896]{1,0:T(8,128)} %copy.23, bf16[768,512]{1,0:T(8,128)(2,1)} %copy-done.5, bf16[768,2688]{1,0:T(8,128)(2,1)} %bitcast.64), kind=kOutput, calls=%fused_computation.11 | convolution fusion | flops 705101824 | bytes 5832704 | tf_op jit(solution)/shard_map/dot_general | solution.py:542
  148.6 1.1 broadcast_in_dim.64
  149.7 3.5 %bitcast_multiply_fusion = f32[896,512]{1,0:T(8,128)} fusion(f32[112,8,4,128]{3,2,1,0:T(4,128)S(1)} %bitcast.75, bf16[768,512]{1,0:T(8,128)(2,1)S(1)} %bitcast.69, bf16[768,2688]{1,0:T(8,128)(2,1)} %bitcast.65), kind=kOutput, calls=%fused_computation.4 | convolution fusion | flops 705101824 | bytes 5832704 | tf_op jit(solution)/shard_map/dot_general | solution.py:544
  153.2 0.6 copy.48
  153.8 0.6 copy.49
  154.4 0.6 copy.50
  (48 shorter events, 1.0 us)
Async XLA Ops:
  0.6 32.9 %copy-start.12 = (s32[4,7]{1,0:T(4,128)S(1)}, s32[4,7]{1,0:T(4,128)}, u32[]{:S(2)}) copy-start(s32[4,7]{1,0:T(4,128)} %param.15) | copy-start | bytes 340
  1.6 0.8 copy-start.1
  2.4 0.8 copy-start.3
  3.2 31.5 %copy-start.7 = (bf16[512,896]{1,0:T(8,128)(2,1)S(1)}, bf16[512,896]{1,0:T(8,128)(2,1)}, u32[]{:S(2)}) copy-start(bf16[512,896]{1,0:T(8,128)(2,1)} %param.11) | copy-start | bytes 2752516
  31.5 6.8 %copy-start.5 = (bf16[768,512]{1,0:T(8,128)(2,1)}, bf16[768,512]{1,0:T(8,128)(2,1)S(1)}, u32[]{:S(2)}) copy-start(bf16[768,512]{1,0:T(8,128)(2,1)S(1)} %fusion.3) | copy-start | bytes 2359300
  36.0 2.3 %copy-start.8 = (bf16[512,7,128]{0,2,1:T(8,128)(2,1)S(1)}, bf16[512,7,128]{0,2,1:T(8,128)(2,1)}, u32[]{:S(2)}) copy-start(bf16[512,7,128]{0,2,1:T(8,128)(2,1)} %broadcast_in_dim.51) | copy-start | bytes 2752516
  38.3 4.9 %copy-start.13 = (s32[7,4]{0,1:T(4,128)S(1)}, s32[7,4]{0,1:T(4,128)}, u32[]{:S(2)}) copy-start(s32[7,4]{0,1:T(4,128)} %param.16) | copy-start | bytes 340
  44.5 2.4 %copy-start.6 = (bf16[768,1792]{1,0:T(8,128)(2,1)S(1)}, bf16[768,1792]{1,0:T(8,128)(2,1)}, u32[]{:S(2)}) copy-start(bf16[768,1792]{1,0:T(8,128)(2,1)} %convolution_convert_fusion) | copy-start | bytes 8257540
  49.1 53.1 %copy-start.9 = (bf16[512,7,128]{0,2,1:T(8,128)(2,1)S(1)}, bf16[512,7,128]{0,2,1:T(8,128)(2,1)}, u32[]{:S(2)}) copy-start(bf16[512,7,128]{0,2,1:T(8,128)(2,1)} %broadcast_in_dim.53) | copy-start | bytes 2752516
  49.1 53.1 %copy-start.10 = (bf16[512,896]{0,1:T(8,128)(2,1)S(1)}, bf16[512,896]{0,1:T(8,128)(2,1)}, u32[]{:S(2)}) copy-start(bf16[512,896]{0,1:T(8,128)(2,1)} %copy.17) | copy-start | bytes 2752516
  49.1 53.1 %copy-start.11 = (bf16[512,896]{0,1:T(8,128)(2,1)S(1)}, bf16[512,896]{0,1:T(8,128)(2,1)}, u32[]{:S(2)}) copy-start(bf16[512,896]{0,1:T(8,128)(2,1)} %copy.18) | copy-start | bytes 2752516
  102.2 1.9 %copy-start = (bf16[4,4,48,2688]{3,2,1,0:T(8,128)(2,1)}, bf16[4,4,48,2688]{3,2,1,0:T(8,128)(2,1)S(1)}, u32[]{:S(2)}) copy-start(bf16[4,4,48,2688]{3,2,1,0:T(8,128)(2,1)S(1)} %exchange_hidden.1) | copy-start | bytes 12386308
  102.2 1.9 %copy-start.14 = (bf16[896,512]{1,0:T(8,128)(2,1)S(1)}, bf16[896,512]{1,0:T(8,128)(2,1)}, u32[]{:S(2)}) copy-start(bf16[896,512]{1,0:T(8,128)(2,1)} %param.13) | copy-start | bytes 2752516
  104.1 1.1 copy-start.2
  104.1 1.1 copy-start.4

commit v2 on v0

v2 whole, which is shorter than its diff:
```python
import jax
import jax.numpy as jnp
from jax import lax
from jax.experimental import pallas as pl
from jax.experimental.pallas import tpu as pltpu
from jax.sharding import PartitionSpec as P

D = 8192
T = 48
W = 512
U = 896
LANES = 3 * U
CHUNKS = ((0, 16), (16, 16), (32, 16))
SKEW = 2
F32 = jnp.float32
BF16 = jnp.bfloat16
MESH = pl.DeviceIdType.MESH
VM = pl.BlockSpec(memory_space=pltpu.VMEM)
SM = pl.BlockSpec(memory_space=pltpu.SMEM)
LAST = (((1,), (1,)), ((), ()))
FIRST = (((0,), (0,)), ((), ()))
PARTS = (((0, 768), (768, 640)), ((1408, 640), (2048, 640)))


def add(*values):
    total = values[0].astype(F32)
    for value in values[1:]:
        total = total + value.astype(F32)
    return total


def peers_of_row(row):
    return [{"row": lax.rem(row + k, 16)} for k in range(1, 16)]


def peers_of_cols(dp, z):
    me = dp * 8 + z
    found = []
    for k in range(1, 16):
        other = lax.rem(me + k, 16)
        found.append({"dp": other // 8, "col": lax.rem(other, 8)})
    return found


def greet(devices):
    barrier = pltpu.get_barrier_semaphore()
    for dev in devices:
        pl.semaphore_signal(barrier, inc=1, device_id=dev, device_id_type=MESH)
    pl.semaphore_wait(barrier, len(devices))


class Sender:
    def __init__(self):
        self.started = []

    def go(self, src, dst, send, recv, dev):
        copy = pltpu.make_async_remote_copy(
            src_ref=src, dst_ref=dst, send_sem=send, recv_sem=recv, device_id=dev, device_id_type=MESH
        )
        copy.start()
        self.started.append(copy)
        return copy

    def drain(self):
        for copy in self.started:
            copy.wait_send()


class Ring:
    def __init__(self, pos, right, left):
        self.here = pos
        self.next = lax.rem(pos + 1, 4)
        self.far = lax.rem(pos + 2, 4)
        self.prev = lax.rem(pos + 3, 4)
        self.right, self.left = right, left


class Scatter:
    def __init__(self, ring, wire, exact, bufs, send, recv, out):
        self.ring, self.wire, self.exact, self.bufs = ring, wire, exact, bufs
        self.send, self.recv, self.out = send, recv, out
        self.copies = {}

    def go(self, k, src, dst, dev):
        self.copies[k] = self.out.go(src, dst, self.send.at[k], self.recv.at[k], dev)

    def begin(self):
        ring, wire, b = self.ring, self.wire, self.bufs
        self.go(0, wire(ring.far, 0), b["hop"][0], ring.right)
        self.go(1, wire(ring.far, 1), b["hop"][1], ring.left)
        self.go(2, wire(ring.next, 1), b["left"][1], ring.right)
        self.go(3, wire(ring.prev, 0), b["right"][0], ring.left)

    def middle(self, part):
        ring, b = self.ring, self.bufs
        self.copies[part].wait_recv()
        piece = self.exact(ring.next if part == 0 else ring.prev, part)
        b["sum"][part][...] = add(piece[...], b["hop"][part][...]).astype(BF16)
        if part == 0:
            self.go(4, b["sum"][0], b["left"][0], ring.right)
        else:
            self.go(5, b["sum"][1], b["right"][1], ring.left)

    def end(self, part):
        b = self.bufs
        for k in ((3, 4), (2, 5))[part]:
            self.copies[k].wait_recv()
        return add(self.exact(self.ring.here, part)[...], b["left"][part][...], b["right"][part][...])


class Spread:
    def __init__(self, ring, slot, send, recv, out):
        self.ring, self.slot = ring, slot
        self.send, self.recv, self.out = send, recv, out
        self.copies = {}

    def go(self, k, ref, dev):
        self.copies[k] = self.out.go(ref, ref, self.send.at[k], self.recv.at[k], dev)

    def begin(self):
        ring, slot = self.ring, self.slot
        self.go(0, slot(ring.here, 0), ring.right)
        self.go(1, slot(ring.here, 1), ring.left)
        self.go(2, slot(ring.here, 1), ring.right)
        self.go(3, slot(ring.here, 0), ring.left)

    def middle(self, part):
        ring, slot = self.ring, self.slot
        self.copies[part].wait_recv()
        if part == 0:
            self.go(4, slot(ring.prev, 0), ring.right)
        else:
            self.go(5, slot(ring.next, 1), ring.left)

    def end(self):
        for k in range(2, 6):
            self.copies[k].wait_recv()


def activation(gate, up_value, hidden_grad):
    s = jax.nn.sigmoid(gate)
    hidden = (gate * s * up_value).astype(BF16)
    gate_grad = (hidden_grad * up_value * s * (1.0 + gate * (1.0 - s))).astype(BF16)
    up_grad = (hidden_grad * gate * s).astype(BF16)
    return hidden, gate_grad, up_grad


def lanes(chain, part):
    start, size = PARTS[chain][part]
    return pl.ds(start, size)


def scratch_plan():
    plan = {
        "x_all": pltpu.VMEM((2, 8, T, W), BF16),
        "c_all": pltpu.VMEM((2, 8, T, W), BF16),
        "sq_buf": pltpu.VMEM((16, 1, 128), F32),
        "inv_buf": pltpu.VMEM((16, 1, 128), F32),
        "dot_buf": pltpu.VMEM((16, 1, 128), F32),
        "gain_buf": pltpu.VMEM((16, 1, W), F32),
        "square": pltpu.VMEM((128, 128), F32),
        "inv_cols": pltpu.VMEM((128, 128), F32),
        "inv_own": pltpu.VMEM((128, 128), F32),
        "w_gu": pltpu.VMEM((W, 2 * U), BF16),
        "w_d": pltpu.VMEM((U, W), BF16),
        "grad_sum": pltpu.VMEM((T, W), F32),
    }
    for c, (_, t) in enumerate(CHUNKS):
        plan[f"nx{c}"] = pltpu.VMEM((16 * t, W), BF16)
        plan[f"pf{c}"] = pltpu.VMEM((4, 4, t, LANES), F32)
        plan[f"pb{c}"] = pltpu.VMEM((4, 4, t, LANES), BF16)
        plan[f"q{c}"] = pltpu.VMEM((4, 4, t, LANES), BF16)
        plan[f"total{c}"] = pltpu.VMEM((t, LANES), F32)
        plan[f"zf{c}"] = pltpu.VMEM((2, 2, 8, t, W), F32)
        plan[f"zb{c}"] = pltpu.VMEM((2, 2, 8, t, W), BF16)
        plan[f"pair{c}"] = pltpu.VMEM((2, 8, t, W), BF16)
        plan[f"go{c}"] = pltpu.VMEM((2, 4, 2, t, W), BF16)
        plan[f"come{c}"] = pltpu.VMEM((2, 4, 2, t, W), BF16)
        for chain in range(2):
            for part in range(2):
                size = PARTS[chain][part][1]
                plan[f"mf{c}{chain}{part}"] = pltpu.VMEM((4, t, size), F32)
                plan[f"mb{c}{chain}{part}"] = pltpu.VMEM((4, t, size), BF16)
                for name in ("hop", "sum", "left", "right"):
                    plan[f"big_{name}{c}{chain}{part}"] = pltpu.VMEM((4, t, size), BF16)
                    plan[f"small_{name}{c}{chain}{part}"] = pltpu.VMEM((t, size), BF16)
    n = len(CHUNKS)
    for name, shape in (
        ("row", (n, 2, 4, 6)), ("ring", (2, 4, 2)), ("mate", (8, 2)), ("sq", (15,)), ("inv", (15,)),
        ("pairs", (n, 2)), ("zring", (n, 2, 4, 2)), ("dot", (15,)), ("gain", (15,)),
    ):
        plan[name + "_send"] = pltpu.SemaphoreType.DMA(shape)
        plan[name + "_recv"] = pltpu.SemaphoreType.DMA(shape)
    return plan


PLAN = scratch_plan()


def kernel(
    tok, cot, gain, gate_w, up_w, down_w, keep_gu, keep_d,
    branch_out, tokens_out, gain_out, gu_out, d_out, *scratch,
):
    s = dict(zip(PLAN, scratch))
    dp, row, z = lax.axis_index("dp"), lax.axis_index("row"), lax.axis_index("col")
    me = dp * 8 + z
    px, py = row // 4, lax.rem(row, 4)
    row_peers, col_peers = peers_of_row(row), peers_of_cols(dp, z)
    right, left = {"col": lax.rem(z + 1, 8)}, {"col": lax.rem(z + 7, 8)}
    mate = {"dp": 1 - dp}
    out = Sender()
    x_all, c_all = s["x_all"], s["c_all"]
    square = s["square"]

    def as_row(column):
        square[...] = jnp.zeros((128, 128), F32)
        square[pl.ds(0, T), :] = jnp.broadcast_to(column, (T, 128))
        return jnp.transpose(square[...])[0:1]

    token_f = tok[...].astype(F32)
    x_all[dp, z] = tok[...]
    c_all[dp, z] = cot[...]
    s["sq_buf"][row] = as_row(jnp.sum(token_f * token_f, axis=1, keepdims=True))
    greet(row_peers + col_peers)

    alls = (x_all, c_all)

    def ring(side, step, unit):
        block = lax.rem(z + (9 - step if side == 0 else step + 7), 8)
        here = (tok, cot)[unit] if step == 1 else alls[unit].at[dp, block]
        return out.go(
            here, alls[unit].at[dp, block], s["ring_send"].at[side, step - 1, unit],
            s["ring_recv"].at[side, step - 1, unit], right if side == 0 else left,
        )

    def pair(slot, block, unit, own=False):
        here = (tok, cot)[unit] if own else alls[unit].at[dp, block]
        return out.go(
            here, alls[unit].at[dp, block], s["mate_send"].at[slot, unit], s["mate_recv"].at[slot, unit], mate
        )

    flying, mated = {}, []
    for unit in range(2):
        for side in range(2):
            u = unit if side == 0 else 1 - unit
            flying[side, 1, u] = ring(side, 1, u)
    squared = [
        out.go(
            s["sq_buf"].at[row], s["sq_buf"].at[row], s["sq_send"].at[k], s["sq_recv"].at[k], row_peers[k]
        )
        for k in range(15)
    ]
    for unit in range(2):
        mated.append(pair(0, z, unit, own=True))

    def mask_rows(i):
        rows = pl.ds(pl.multiple_of(i * 128, 128), 128)
        for j in range(14):
            piece = (gate_w, up_w)[j // 7][rows, pl.ds((j % 7) * 128, 128)]
            s["w_gu"][rows, pl.ds(j * 128, 128)] = (piece.astype(F32) * keep_gu[i, j].astype(F32)).astype(BF16)

    def mask_down(i):
        rows = pl.ds(pl.multiple_of(i * 128, 128), 128)
        for j in range(4):
            piece = down_w[rows, pl.ds(j * 128, 128)]
            s["w_d"][rows, pl.ds(j * 128, 128)] = (piece.astype(F32) * keep_d[i, j].astype(F32)).astype(BF16)

    inv_done = []
    for step in range(1, 5):
        for unit in range(2):
            for side in range(2):
                u = unit if side == 0 else 1 - unit
                if step == 4 and u != side:
                    continue
                flying[side, step, u].wait_recv()
                if step < 3 or (step == 3 and u == side):
                    flying[side, step + 1, u] = ring(side, step + 1, u)
                block = lax.rem(z + (8 - step if side == 0 else step), 8)
                mated.append(pair(step if side == 0 or step == 4 else step + 4, block, u))
        if step == 1:
            for copy in squared:
                copy.wait_recv()
            total = s["sq_buf"][0]
            for k in range(1, 16):
                total = total + s["sq_buf"][k]
            inv_row = lax.rsqrt(total / D + 1e-05)
            s["inv_buf"][me] = inv_row
            at = s["inv_buf"].at[me]
            inv_done = [
                out.go(at, at, s["inv_send"].at[k], s["inv_recv"].at[k], col_peers[k]) for k in range(15)
            ]
            s["inv_own"][...] = jnp.transpose(jnp.broadcast_to(inv_row, (128, 128)))
        if step == 2:
            @pl.loop(0, 4)
            def _(i):
                mask_rows(i)
        if step == 3:
            @pl.loop(0, 7)
            def _(i):
                mask_down(i)
    for copy in inv_done:
        copy.wait_recv()
    square[...] = jnp.zeros((128, 128), F32)
    for b in range(16):
        square[pl.ds(b, 1), :] = s["inv_buf"][b]
    s["inv_cols"][...] = jnp.transpose(square[...])
    for copy in mated:
        copy.wait_recv()

    def at(x, y):
        return {"row": x * 4 + y}

    rings = (
        Ring(px, at(lax.rem(px + 1, 4), py), at(lax.rem(px + 3, 4), py)),
        Ring(py, at(px, lax.rem(py + 1, 4)), at(px, lax.rem(py + 3, 4))),
    )

    def pieces(ref, chain):
        if chain == 0:
            return lambda d, part: ref.at[d, :, :, lanes(chain, part)]
        return lambda d, part: ref.at[:, d, :, lanes(chain, part)]

    def project(c):
        r0, t = CHUNKS[c]
        nx, pf, pb = s[f"nx{c}"], s[f"pf{c}"], s[f"pb{c}"]
        for b in range(16):
            value = x_all[b // 8, b % 8, pl.ds(r0, t), :].astype(F32)
            inv = s["inv_cols"][pl.ds(r0, t), b : b + 1]
            nx[pl.ds(b * t, t), :] = (value * inv * gain[...]).astype(BF16)

        @pl.loop(0, 7)
        def _(j):
            wide = pl.ds(pl.multiple_of(j * 256, 256), 256)
            value = jnp.dot(nx[...], s["w_gu"][:, wide], preferred_element_type=F32).reshape(4, 4, t, 256)
            pf[:, :, :, wide] = value
            pb[:, :, :, wide] = value.astype(BF16)
            seen = c_all[:, :, pl.ds(r0, t), :].reshape(16 * t, W)
            rows = pl.ds(pl.multiple_of(j * 128, 128), 128)
            value = lax.dot_general(seen, s["w_d"][rows, :], LAST, preferred_element_type=F32)
            value = value.reshape(4, 4, t, 128)
            narrow = pl.ds(pl.multiple_of(2 * U + j * 128, 128), 128)
            pf[:, :, :, narrow] = value
            pb[:, :, :, narrow] = value.astype(BF16)

    def flow(c):
        r0, t = CHUNKS[c]
        q, total = s[f"q{c}"], s[f"total{c}"]

        def bufs(size, chain):
            return {
                name: [s[f"{size}_{name}{c}{chain}{part}"] for part in range(2)]
                for name in ("hop", "sum", "left", "right")
            }

        def sems(chain, stage):
            return s["row_send"].at[c, chain, stage], s["row_recv"].at[c, chain, stage]

        project(c)
        one = [
            Scatter(
                rings[k], pieces(s[f"pb{c}"], k), pieces(s[f"pf{c}"], k), bufs("big", k), *sems(k, 0), out
            )
            for k in range(2)
        ]
        for k in range(2):
            one[k].begin()
        yield
        for part in range(2):
            for k in range(2):
                one[k].middle(part)
        yield
        two = []
        for k in range(2):
            exact = [s[f"mf{c}{k}{part}"] for part in range(2)]
            wire = [s[f"mb{c}{k}{part}"] for part in range(2)]
            for part in range(2):
                value = one[k].end(part)
                exact[part][...] = value
                wire[part][...] = value.astype(BF16)
            two.append(
                Scatter(
                    rings[1 - k], lambda d, part, wire=wire: wire[part].at[d],
                    lambda d, part, exact=exact: exact[part].at[d], bufs("small", k), *sems(k, 1), out,
                )
            )
            two[k].begin()
        yield
        for part in range(2):
            for k in range(2):
                two[k].middle(part)
        yield
        for k in range(2):
            for part in range(2):
                total[:, lanes(k, part)] = two[k].end(part)
        values = activation(total[:, pl.ds(0, U)], total[:, pl.ds(U, U)], total[:, pl.ds(2 * U, U)])
        for i in range(3):
            q[px, py, :, pl.ds(i * U, U)] = values[i]

        def near(k):
            if k == 0:
                return lambda d, part: q.at[px, d, :, lanes(k, part)]
            return lambda d, part: q.at[d, py, :, lanes(k, part)]

        three = [Spread(rings[1 - k], near(k), *sems(k, 2), out) for k in range(2)]
        four = [Spread(rings[k], pieces(q, k), *sems(k, 3), out) for k in range(2)]
        for k in range(2):
            three[k].begin()
        yield
        for part in range(2):
            for k in range(2):
                three[k].middle(part)
        yield
        for k in range(2):
            three[k].end()
            four[k].begin()
        yield
        for part in range(2):
            for k in range(2):
                four[k].middle(part)
        yield
        for k in range(2):
            four[k].end()

        zf, zb, pair_buf = s[f"zf{c}"], s[f"zb{c}"], s[f"pair{c}"]
        go_buf, come_buf = s[f"go{c}"], s[f"come{c}"]
        paired = []
        for unit in range(2):
            @pl.loop(0, 4)
            def _(j, unit=unit):
                part = pl.ds(pl.multiple_of(j * 128, 128), 128)
                if unit == 0:
                    seen = q[:, :, :, pl.ds(0, U)].reshape(16 * t, U)
                    value = jnp.dot(seen, s["w_d"][:, part], preferred_element_type=F32)
                else:
                    seen = q[:, :, :, pl.ds(U, 2 * U)].reshape(16 * t, 2 * U)
                    value = lax.dot_general(seen, s["w_gu"][part, :], LAST, preferred_element_type=F32)
                value = value.reshape(2, 8, t, 128)
                zf[unit, :, :, :, part] = value
                zb[unit, :, :, :, part] = value.astype(BF16)

            paired.append(
                out.go(
                    zb.at[unit, 1 - dp], pair_buf.at[unit], s["pairs_send"].at[c, unit],
                    s["pairs_recv"].at[c, unit], mate,
                )
            )
        yield

        def mine(off, unit):
            dest = lax.rem(z + off, 8)
            return add(zf[unit, dp, dest], pair_buf[unit, dest])

        for copy in paired:
            copy.wait_recv()
        hops = {}
        for step in range(1, 5):
            for unit in range(2):
                for side in range(2):
                    u = unit if side == 0 else 1 - unit
                    if step == 1 and u != side:
                        continue
                    value = mine(5 - step if side == 0 else 3 + step, u)
                    if step > 2 or (step == 2 and u == side):
                        hops[side, step - 1, u].wait_recv()
                        value = value + come_buf[side, step - 2, u].astype(F32)
                    go_buf[side, step - 1, u] = value.astype(BF16)
                    hops[side, step, u] = out.go(
                        go_buf.at[side, step - 1, u], come_buf.at[side, step - 1, u],
                        s["zring_send"].at[c, side, step - 1, u], s["zring_recv"].at[c, side, step - 1, u],
                        right if side == 0 else left,
                    )
            yield
        for unit in range(2):
            value = mine(0, unit)
            for side in range(2):
                hops[side, 4, unit].wait_recv()
                value = value + come_buf[side, 3, unit].astype(F32)
            if unit == 0:
                branch_out[pl.ds(r0, t), :] = value.astype(BF16)
            else:
                s["grad_sum"][pl.ds(r0, t), :] = value

    def weight_grads():
        for start, size in ((0, 4), (4, 3)):
            @pl.loop(start, start + size)
            def _(j):
                wide = pl.ds(pl.multiple_of(j * 256, 256), 256)
                from_q = pl.ds(pl.multiple_of(U + j * 256, 128), 256)
                value = jnp.zeros((W, 256), F32)
                for c, (_, t) in enumerate(CHUNKS):
                    value = value + lax.dot_general(
                        s[f"nx{c}"][...], s[f"q{c}"][:, :, :, from_q].reshape(16 * t, 256), FIRST,
                        preferred_element_type=F32,
                    )
                for i in range(4):
                    for h in range(2):
                        gu_out[pl.ds(i * 128, 128), pl.ds(pl.multiple_of(j * 256 + h * 128, 128), 128)] = (
                            value[i * 128 : i * 128 + 128, h * 128 : h * 128 + 128]
                            * keep_gu[i, 2 * j + h].astype(F32)
                        )
            yield

        @pl.loop(0, 7)
        def _(j):
            rows = pl.ds(pl.multiple_of(j * 128, 128), 128)
            value = jnp.zeros((128, W), F32)
            for c, (r0, t) in enumerate(CHUNKS):
                value = value + lax.dot_general(
                    s[f"q{c}"][:, :, :, rows].reshape(16 * t, 128),
                    c_all[:, :, pl.ds(r0, t), :].reshape(16 * t, W), FIRST, preferred_element_type=F32,
                )
            for i in range(4):
                d_out[rows, pl.ds(i * 128, 128)] = value[:, i * 128 : i * 128 + 128] * keep_d[j, i].astype(F32)
        yield

    n = len(CHUNKS)
    flows = [flow(c) for c in range(n)]
    grads = weight_grads()
    live = set(range(n))
    slot = 0
    while live:
        for c in range(n):
            if c in live and slot >= SKEW * c:
                try:
                    next(flows[c])
                except StopIteration:
                    live.discard(c)
        if slot >= SKEW * (n - 1) + 9:
            next(grads, None)
        slot += 1
    for _ in grads:
        pass

    normed_grad = s["grad_sum"][...]
    token_f = tok[...].astype(F32)
    inv_rms = s["inv_own"][pl.ds(0, T), 0:1]
    weighted = normed_grad * token_f
    s["gain_buf"][me] = jnp.sum(weighted * inv_rms, axis=0, keepdims=True)
    s["dot_buf"][row] = as_row(jnp.sum(gain[...] * weighted, axis=1, keepdims=True))
    small = []
    for k in range(15):
        at_row, at_me = s["dot_buf"].at[row], s["gain_buf"].at[me]
        small.append(out.go(at_row, at_row, s["dot_send"].at[k], s["dot_recv"].at[k], row_peers[k]))
        small.append(out.go(at_me, at_me, s["gain_send"].at[k], s["gain_recv"].at[k], col_peers[k]))
    for copy in small:
        copy.wait_recv()
    inner, gain_total = s["dot_buf"][0], s["gain_buf"][0]
    for k in range(1, 16):
        inner = inner + s["dot_buf"][k]
        gain_total = gain_total + s["gain_buf"][k]
    gain_out[...] = gain_total
    square[...] = jnp.transpose(jnp.broadcast_to(inner, (128, 128)))
    inner_col = square[pl.ds(0, T), 0:1]
    tokens_out[...] = inv_rms * gain[...] * normed_grad - token_f * inv_rms * inv_rms * inv_rms * inner_col / D
    out.drain()


def on_device(
    tokens, norm_gain, gate_weight, up_weight, down_weight, gate_keep, up_keep, down_keep, cotangent
):
    branch, grad_tokens, grad_gain, grad_gu, grad_down = pl.pallas_call(
        kernel,
        out_shape=(
            jax.ShapeDtypeStruct((T, W), BF16),
            jax.ShapeDtypeStruct((T, W), F32),
            jax.ShapeDtypeStruct((1, W), F32),
            jax.ShapeDtypeStruct((W, 2 * U), F32),
            jax.ShapeDtypeStruct((U, W), F32),
        ),
        in_specs=[VM] * 6 + [SM] * 2,
        out_specs=(VM,) * 5,
        scratch_shapes=list(PLAN.values()),
        compiler_params=pltpu.CompilerParams(
            collective_id=0, has_side_effects=True, vmem_limit_bytes=60 * 1024 * 1024
        ),
        name="feed_forward",
    )(
        tokens, cotangent, norm_gain[None, :], gate_weight, up_weight, down_weight,
        jnp.concatenate([gate_keep, up_keep], axis=1), down_keep,
    )
    return branch, grad_tokens, grad_gain[0], grad_gu[:, :U], grad_gu[:, U:], grad_down


def solution(mesh):
    wide = P("row", ("dp", "col"))
    tall = P(("dp", "col"), "row")
    return jax.shard_map(
        on_device,
        mesh=mesh,
        in_specs=(tall, P("row"), wide, wide, tall, wide, wide, tall, tall),
        out_specs=(tall, tall, P("row"), wide, wide, tall),
        check_vma=False,
    )
```

time: 620 us -> 133 us (0.21)
  waiting for transfers between devices: 388 us -> 0 us
  blocking collectives: 150 us -> 0 us
  Pallas kernels: 0 us -> 122 us
  matrix products: 26.8 us -> 0 us
  other arithmetic: 21.5 us -> 1.35 us
  between operations: 14.8 us -> 0.68 us
  local copies, waits for them, and re-layouts: 17 us -> 8.7 us
    unnamed x15 -> x0, waiting for transfers between devices: 190 us -> none
    all_gather x6 -> x0, waiting for transfers between devices: 143 us -> none  [the longest x1 48.1 us: on_device(): lax.all_gather(up_grad, 'row', axis=0, tiled=True)]
    pallas_call x0 -> x1, Pallas kernels: none -> 122 us  [on_device(): pl.pallas_call(kernel, out_shape=(jax.ShapeDtypeStruct((T, W), BF16), jax...]
    psum x3 -> x0, blocking collectives: 108 us -> none  [the longest x1 40.5 us: on_device(): lax.psum(jnp.sum(normed_grad * token_f * inv_rms, axis=0), ('dp', 'col'))]
    reduce_scatter x5 -> x0, waiting for transfers between devices: 55.3 us -> none  [the longest x1 37.9 us: on_device(): lax.psum_scatter(lax.dot_general(gate_grads, gate_full, contract_last, pr...]
    all_gather x2 -> x0, blocking collectives: 42.1 us -> none  [the longest x1 22.6 us: on_device(): seen_rows = lax.all_gather(normed, 'col', axis=0, tiled=True)]
    dot_general x9 -> x0, matrix products: 26.8 us -> none  [the longest x1 4.28 us: on_device(): lax.dot_general(seen_rows, gate_grads, contract_first, preferred_element_...]
    mul x6 -> x0, other arithmetic: 11.2 us -> none  [the longest x1 3.6 us: on_device(): grad_gate = gate_total * expand_keep(gate_keep, jnp.float32)]
  transfers between devices with their start and end apart: 13 -> 0, of which waited for: 7 -> 0; matrix products, arithmetic and copies ran while one was open for 8% -> 0% of each run, Pallas kernels for 0% -> 0%
where the time goes in v2:
time: 133 us
  Pallas kernels  122 us (92%)
  local copies, waits for them, and re-layouts  8.7 us (7%)
  other arithmetic  1.35 us (1%)
    pallas_call x1, Pallas kernels, on_device(): pl.pallas_call(kernel, out_shape=(jax.ShapeDtypeStruct((T, W), BF16), jax...  122 us
    unnamed x13, local copies, waits for them, and re-layouts  4.44 us
    slice x1, local copies, waits for them, and re-layouts, on_device(): grad_gu[:, U:]  4.26 us

profile of v2, /device:TPU:1, one launch (start us, length us, event | category | flops | bytes accessed | tf_op | source)
XLA Modules:
  0.0 132.6 jit_solution(9527364349598107009)
XLA Ops:
  0.6 1.4 %pad_add_fusion.keep_gu = s32[4,14]{1,0:T(4,128)} fusion(s32[4,7]{1,0:T(4,128)} %param.15, s32[4,7]{1,0:T(4,128)} %param.14), kind=kLoop, calls=%fused_computation | loop fusion | flops 56 | bytes 448 | tf_op jit(solution)/shard_map/concatenate | solution.py:579
  2.0 1.4 %copy.15.keep_d = s32[7,4]{1,0:T(8,128)} copy(s32[7,4]{0,1:T(4,128)} %param.16) | data formatting | bytes 224 | tf_op args[7]
  3.3 121.9 %feed_forward.1 = (bf16[48,512]{1,0:T(8,128)(2,1)}, f32[48,512]{1,0:T(8,128)}, f32[1,512]{1,0:T(1,128)}, f32[512,1792]{1,0:T(8,128)}, f32[896,512]{1,0:T(8,128)}) custom-call(bf16[48,512]{1,0:T(8,128)(2,1)} %tok.1, bf16[48,512]{1,0:T(8,128)(2,1)} %cot.1, f32[1,512]{1,0:T(1,128)} %bitcast.3, bf16[512,896]{1,0:T(8,128)(2,1)} %gate_w.1, bf16[512,896]{1,0:T(8,128)(2,1)} %up_w.1, ...), custom_call_target="tpu_custom_call" | custom-call | tf_op jit(solution)/shard_map/feed_forward/pallas_call | solution.py:561
  125.2 0.0 copy-start.2
  125.2 0.0 copy-start.1
  125.2 0.0 copy-start.3
  125.2 0.0 copy-start
  125.2 4.3 %fusion = (f32[512,896]{1,0:T(8,128)}, f32[512,896]{1,0:T(8,128)}) fusion(f32[512,1792]{1,0:T(8,128)} %get-tuple-element.14), kind=kLoop, calls=%fused_computation.1 | loop fusion | bytes 7340032 | tf_op jit(solution)/shard_map/slice | solution.py:581
  129.5 0.0 copy-done.2
  129.5 0.6 copy.20
  130.1 0.0 copy-done.1
  130.1 0.6 copy.21
  130.8 0.0 copy-done.3
  130.8 0.6 copy.22
  131.4 0.0 copy-done
  131.4 1.2 copy.23
Async XLA Ops:
  125.2 4.3 %copy-start.2 = (bf16[48,512]{1,0:T(8,128)(2,1)S(1)}, bf16[48,512]{1,0:T(8,128)(2,1)}, u32[]{:S(2)}) copy-start(bf16[48,512]{1,0:T(8,128)(2,1)} %get-tuple-element.24) | copy-start | bytes 147460
  125.2 4.9 %copy-start.1 = (f32[48,512]{1,0:T(8,128)S(1)}, f32[48,512]{1,0:T(8,128)}, u32[]{:S(2)}) copy-start(f32[48,512]{1,0:T(8,128)} %get-tuple-element.25) | copy-start | bytes 294916
  125.2 5.6 %copy-start.3 = (f32[1,512]{1,0:T(1,128)S(1)}, f32[1,512]{1,0:T(1,128)}, u32[]{:S(2)}) copy-start(f32[1,512]{1,0:T(1,128)} %get-tuple-element.13) | copy-start | bytes 6148
  125.2 6.1 %copy-start = (f32[896,512]{1,0:T(8,128)S(1)}, f32[896,512]{1,0:T(8,128)}, u32[]{:S(2)}) copy-start(f32[896,512]{1,0:T(8,128)} %get-tuple-element.29) | copy-start | bytes 5505028
